TPU v7x, 32 devices: a whole 2x2x4 slice. The times are simulated.
32 devices in a mesh: blk: 8 (over y, x, core), wide: 4 (over z).
Axes of the slice: x: 2, y: 2, z: 4, core: 2. Of those that a mesh axis runs over, the one named last changes fastest.
Arguments:
- coupling: bfloat16 [1024, 8, 2, 512], P('blk', 'wide'), may hold values from -0.09375 to 0.09375
- rp_cells: int32 [3, 1024], replicated, may hold values from -8 to 7
- re_cells: int32 [3, 8], P(None, 'wide'), may hold values from -8 to 7
- q_points: int32 [3, 2048], P(None, 'blk'), may hold values from 0 to 31
- k_points: int32 [3, 2], replicated, may hold values from 0 to 31
- mode_energy: float32 [16, 2048], P(None, 'blk'), may hold values from 0.02 to 1
Outputs:
- bloch_coupling: float32 [2, 2, 512, 2048], P(None, None, 'wide', 'blk')
All inputs are finite; a program needn't handle non-finite values.
Results may differ from a plain program's by a relative error of at most 0.002.
Values may be sent and summed in bfloat16 or wider, within the bound.
No kernel may reach another device: no remote copies, remote signals or barrier semaphores. Data moves between devices by JAX's collectives and lax.ppermute only.
A program may use at most 64 MiB of HBM per device.

v0:
```python
import math
import jax
import jax.numpy as jnp
from jax import lax
from jax.sharding import PartitionSpec as P

MODES = 16
MESHQ = 32
MESHK = 32


def phase_parts(left, right, modulus):
    whole = jnp.sum(left[:, :, None] * right[:, None, :], axis=0)
    angle = jnp.mod(whole, modulus).astype(jnp.float32) * (2.0 * math.pi / modulus)
    return (jnp.cos(angle), jnp.sin(angle))


def q_table(q_points, vectors):
    cosine, sine = phase_parts(q_points, vectors, MESHQ)
    return jnp.concatenate([cosine, sine], axis=0).astype(jnp.bfloat16)


def entry_weights(mode_energy, offset, entries):
    weight = 1.0 / jnp.sqrt(2.0 * mode_energy)
    entry_index = offset + jnp.arange(entries, dtype=jnp.int32)
    selector = (
        (entry_index % MODES)[:, None] == jnp.arange(MODES, dtype=jnp.int32)[None, :]
    ).astype(jnp.float32)
    return jnp.dot(selector, weight, precision=lax.Precision.HIGHEST)


def on_device(coupling, rp_cells, re_cells, q_points, k_points, mode_energy):
    slab_rows = coupling.shape[0]
    q_local = q_points.shape[1]
    high = lax.Precision.HIGHEST
    moved = lax.all_to_all(coupling, "wide", split_axis=3, concat_axis=1, tiled=True)
    cells = lax.all_gather(re_cells, "wide", axis=1, tiled=True)
    entries = moved.shape[3]
    offset = lax.axis_index("wide") * entries
    cell_count = moved.shape[1]
    flat = moved.reshape(slab_rows, cell_count * 2 * entries)
    table = q_table(q_points, rp_cells)
    summed = lax.dot_general(
        lax.all_gather(flat, "blk", axis=0, tiled=True),
        table,
        (((0,), (1,)), ((), ())),
        preferred_element_type=jnp.float32,
    )
    summed = summed.reshape(cell_count, 2, entries, 2, q_local)
    real = summed[:, 0, :, 0] - summed[:, 1, :, 1]
    imag = summed[:, 1, :, 0] + summed[:, 0, :, 1]
    entry_weight = entry_weights(mode_energy, offset, entries)
    real = real * entry_weight[None]
    imag = imag * entry_weight[None]
    k_cos, k_sin = phase_parts(k_points, cells, MESHK)
    part_re = jnp.einsum("kr,req->keq", k_cos, real, precision=high) - jnp.einsum(
        "kr,req->keq", k_sin, imag, precision=high
    )
    part_im = jnp.einsum("kr,req->keq", k_cos, imag, precision=high) + jnp.einsum(
        "kr,req->keq", k_sin, real, precision=high
    )
    partial_value = jnp.stack([part_re, part_im], axis=1)
    return partial_value


def solution(mesh):
    in_specs = (
        P("blk", "wide", None, None),
        P(),
        P(None, "wide"),
        P(None, "blk"),
        P(),
        P(None, "blk"),
    )
    out_specs = P(None, None, "wide", "blk")
    return jax.shard_map(
        on_device, mesh=mesh, in_specs=in_specs, out_specs=out_specs, check_vma=False
    )
```

profile of v0, /device:TPU:0, one launch (start us, length us, event | category | flops | bytes accessed | tf_op | source)
XLA Modules:
  0.0 106.6 jit_solution(10636870011201941082)
XLA Ops:
  6.6 2.4 %copy.42 = bf16[128,2,2,512]{0,2,1,3:T(2,128)(2,1)S(1)} copy(bf16[128,2,2,512]{3,2,1,0:T(2,128)(2,1)} %param.6) | data formatting | bytes 1048576 | tf_op args[0]
  9.0 20.6 %all_to_all.15 = bf16[128,2,2,512]{0,2,1,3:T(2,128)(2,1)S(1)} all-to-all(bf16[128,2,2,512]{0,2,1,3:T(2,128)(2,1)S(1)} %copy.42), channel_id=1, replica_groups=mesh['blk'=8,'wide'=4] {'wide'}, dimensions={3} | all-to-all | bytes 1048576 | tf_op jit(solution)/shard_map/all_to_all | solution.py:36
  29.7 0.8 copy.44
  30.5 9.0 %all-gather = s32[4,2,3]{2,1,0:T(2,128)S(1)} all-gather(s32[1,2,3]{2,1,0:T(2,128)S(1)} %bitcast.40), channel_id=1, replica_groups=mesh['blk'=8,'wide'=4] {'wide'}, dimensions={0}, use_global_device_ids=true | all-gather | bytes 120 | tf_op jit(solution)/shard_map/all_gather | solution.py:37
  39.6 0.1 copy.41
  39.7 0.1 copy.40
  39.8 0.1 multiply_reduce_fusion.1
  40.0 0.3 multiply_reduce_fusion
  40.3 0.3 fusion.10
  40.5 4.2 %cosine_convert_fusion = (bf16[256,1024]{1,0:T(8,128)(2,1)S(1)}, bf16[256,1024]{1,0:T(8,128)(2,1)S(1)}) fusion(s32[256,1024]{1,0:T(8,128)S(1)} %multiply_reduce_fusion), kind=kLoop, calls=%fused_computation.18 | loop fusion | flops 3932160 | bytes 2097152 | tf_op jit(solution)/shard_map/convert
  44.8 22.4 %all-gather.3.cloned.1.call-done = bf16[1024,2048]{0,1:T(8,128)(2,1)} async-done(((bf16[128,2048]{0,1:T(8,128)(2,1)}), bf16[1024,2048]{0,1:T(8,128)(2,1)}) %all-gather.3.cloned.1.call-update) | async-done | bytes 4194320 | tf_op jit(solution)/shard_map/all_gather | solution.py:44
  67.1 6.5 %convolution_bitcast_fusion = f32[2048,512]{0,1:T(8,128)} fusion(bf16[1024,2048]{0,1:T(8,128)(2,1)} %all-gather.3.cloned.1.call-done, bf16[256,1024]{1,0:T(8,128)(2,1)S(1)} %get-tuple-element.12, bf16[256,1024]{1,0:T(8,128)(2,1)S(1)} %get-tuple-element.11), kind=kOutput, calls=%fused_computation | convolution fusion | flops 2149580800 | bytes 9437184 | tf_op jit(solution)/shard_map/dot_general | solution.py:43
  73.7 6.6 %reshape.30 = f32[8,2,128,2,256]{2,1,0,4,3:T(2,128)} reshape(f32[2048,512]{0,1:T(8,128)} %convolution_bitcast_fusion) | data formatting | bytes 8388608 | tf_op jit(solution)/shard_map/reshape | solution.py:49
  80.3 8.1 %fusion.27 = (f32[8,1,128,1,256]{2,1,0,4,3:T(1,128)S(1)}, f32[8,1,128,1,256]{2,1,0,4,3:T(1,128)}, f32[8,1,128,1,256]{2,1,0,4,3:T(1,128)S(1)}, f32[8,1,128,1,256]{2,1,0,4,3:T(1,128)}) fusion(f32[8,2,128,2,256]{2,1,0,4,3:T(2,128)} %reshape.30), kind=kLoop, calls=%fused_computation.46 | loop fusion | bytes 8388608 | tf_op jit(solution)/shard_map/slice | solution.py:50
  88.4 0.6 copy.50
  89.0 0.6 copy.51
  89.6 1.6 %copy.52 = f32[8,1,128,1,256]{4,0,2,3,1:T(8,128)S(1)} copy(f32[8,1,128,1,256]{2,1,0,4,3:T(1,128)} %get-tuple-element.8) | data formatting | bytes 2097152
  91.2 2.3 %copy.53 = f32[8,1,128,1,256]{4,0,2,3,1:T(8,128)} copy(f32[8,1,128,1,256]{2,1,0,4,3:T(1,128)} %get-tuple-element.10) | data formatting | bytes 2097152
  93.5 1.0 fusion.8
  94.5 2.2 %fusion.9 = f32[2,128,256]{2,0,1:T(2,128)S(1)} fusion(f32[8,1,128,1,256]{4,0,2,3,1:T(8,128)S(1)} %copy.52, f32[8,1,128,1,256]{4,0,2,3,1:T(8,128)} %copy.53, f32[128,256]{1,0:T(8,128)S(1)} %fusion.10, f32[2,8]{1,0:T(2,128)S(1)} %cos.6), kind=kOutput, calls=%fused_computation.21 | convolution fusion | flops 6815744 | bytes 2490432 | tf_op jit(solution)/shard_map/kr,req->keq/dot_general | solution.py:59
  96.7 1.0 fusion.1
  97.7 1.0 fusion
  98.7 0.2 pad_maximum_fusion
  98.9 0.8 copy.49
  (18 shorter events, 0.2 us)
Async XLA Ops:
  6.5 24.0 %copy-start.4 = (s32[3,2]{0,1:T(2,128)S(1)}, s32[3,2]{0,1:T(2,128)}, u32[]{:S(2)}) copy-start(s32[3,2]{0,1:T(2,128)} %param.8) | copy-start | bytes 76
  6.5 33.1 %copy-start.5 = (s32[3,2]{0,1:T(2,128)S(1)}, s32[3,2]{0,1:T(2,128)}, u32[]{:S(2)}) copy-start(s32[3,2]{0,1:T(2,128)} %param.10) | copy-start | bytes 76
  6.5 33.4 %copy-start.1 = (s32[3,1024]{1,0:T(4,128)S(1)}, s32[3,1024]{1,0:T(4,128)}, u32[]{:S(2)}) copy-start(s32[3,1024]{1,0:T(4,128)} %param.7) | copy-start | bytes 36868
  6.5 33.4 %copy-start.3 = (s32[3,256]{1,0:T(4,128)S(1)}, s32[3,256]{1,0:T(4,128)}, u32[]{:S(2)}) copy-start(s32[3,256]{1,0:T(4,128)} %param.9) | copy-start | bytes 9220
  6.5 33.7 %copy-start.2 = (f32[16,256]{1,0:T(8,128)S(1)}, f32[16,256]{1,0:T(8,128)}, u32[]{:S(2)}) copy-start(f32[16,256]{1,0:T(8,128)} %param.11) | copy-start | bytes 49156
  6.5 60.6 %all-gather.3.cloned.1.call-start = ((), (), s32[]{:S(2)}) async-start(), calls=%async_computation.1 | async-start | bytes 4718592 | tf_op jit(solution)/shard_map/all_gather | solution.py:44
  93.5 3.2 %copy-start = (f32[8,1,128,1,256]{4,0,2,3,1:T(8,128)S(1)}, f32[8,1,128,1,256]{4,0,2,3,1:T(8,128)}, u32[]{:S(2)}) copy-start(f32[8,1,128,1,256]{4,0,2,3,1:T(8,128)} %copy.53) | copy-start | bytes 3145732
Sparse Core Ops, SparseCore 0:
  30.6 36.4 all-gather.2
where the time goes:
time: 107 us
  blocking collectives  29.7 us (28%)
  local copies, waits for them, and re-layouts  24.1 us (23%)
  waiting for transfers between devices  22.4 us (21%)
  between operations  13.6 us (13%)
  matrix products  12 us (11%)
  other arithmetic  4.91 us (5%)
    all_gather x1, waiting for transfers between devices, on_device(): lax.all_gather(flat, 'blk', axis=0, tiled=True)  22.4 us
    all_to_all x1, blocking collectives, on_device(): lax.all_to_all(coupling, 'wide', split_axis=3, concat_axis=1, tiled=True)  20.6 us
    all_gather x1, blocking collectives, on_device(): cells = lax.all_gather(re_cells, 'wide', axis=1, tiled=True)  9.04 us
    slice x1, local copies, waits for them, and re-layouts, on_device(): real = summed[:, 0, :, 0] - summed[:, 1, :, 1]  8.14 us
    unnamed x19, local copies, waits for them, and re-layouts  7.58 us
    reshape x1, local copies, waits for them, and re-layouts, on_device(): summed = summed.reshape(cell_count, 2, entries, 2, q_local)  6.59 us
    dot_general x1, matrix products, on_device(): lax.dot_general(lax.all_gather(flat, 'blk', axis=0, tiled=True), table, (...  6.53 us
    another operation x1, other arithmetic  4.24 us
  transfers between devices with their start and end apart: 1, of which 1 were waited for; matrix products, arithmetic and copies ran while one was open for 5% of the time, Pallas kernels for 0%

commit v1 on v0

--- a/solution.py
+++ b/solution.py
@@ -33,7 +33,10 @@
     slab_rows = coupling.shape[0]
     q_local = q_points.shape[1]
     high = lax.Precision.HIGHEST
-    moved = lax.all_to_all(coupling, "wide", split_axis=3, concat_axis=1, tiled=True)
+    moved = jnp.concatenate(
+        lax.all_to_all(jnp.stack(jnp.split(coupling, lax.axis_size("wide"), axis=3)), "wide", 0, 0),
+        axis=1,
+    )
     cells = lax.all_gather(re_cells, "wide", axis=1, tiled=True)
     entries = moved.shape[3]
     offset = lax.axis_index("wide") * entries

time: 107 us -> 102 us (0.953)
  local copies, waits for them, and re-layouts: 24.1 us -> 15.5 us
  matrix products: 12 us -> 15.2 us
    unnamed x19 -> x16, local copies, waits for them, and re-layouts: 7.58 us -> 0.72 us
    slice x1, local copies, waits for them, and re-layouts: 8.14 us -> 6.56 us  [on_device(): real = summed[:, 0, :, 0] - summed[:, 1, :, 1]]
    split x0 -> x1, local copies, waits for them, and re-layouts: none -> 1.47 us  [on_device(): jnp.split(coupling, lax.axis_size('wide'), axis=3)]
    dot_general x1, matrix products: 0.99 us -> 2.08 us  [on_device(): jnp.einsum('kr,req->keq', k_cos, real, precision=high)]
    dot_general x1, matrix products: 1 us -> 2.09 us  [on_device(): jnp.einsum('kr,req->keq', k_sin, imag, precision=high)]
    dot_general x1, matrix products: 1 us -> 2.09 us  [on_device(): jnp.einsum('kr,req->keq', k_sin, real, precision=high)]
    another operation x1 -> x2, other arithmetic: 4.24 us -> 4.31 us
where the time goes in v1:
time: 102 us; the launch traced here: 101 us
  blocking collectives  29.8 us (29%)
  waiting for transfers between devices  22.4 us (22%)
  local copies, waits for them, and re-layouts  15.5 us (15%)
  matrix products  15.2 us (15%)
  between operations  13.6 us (13%)
  other arithmetic  4.98 us (5%)
    all_gather x1, waiting for transfers between devices, on_device(): lax.all_gather(flat, 'blk', axis=0, tiled=True)  22.4 us
    all_to_all x1, blocking collectives, on_device(): lax.all_to_all(jnp.stack(jnp.split(coupling, lax.axis_size('wide'), axis=...  20.7 us
    all_gather x1, blocking collectives, on_device(): cells = lax.all_gather(re_cells, 'wide', axis=1, tiled=True)  9.04 us
    dot_general x1, matrix products, on_device(): lax.dot_general(lax.all_gather(flat, 'blk', axis=0, tiled=True), table, (...  6.59 us
    slice x1, local copies, waits for them, and re-layouts, on_device(): real = summed[:, 0, :, 0] - summed[:, 1, :, 1]  6.56 us
    reshape x1, local copies, waits for them, and re-layouts, on_device(): summed = summed.reshape(cell_count, 2, entries, 2, q_local)  5.88 us
    another operation x1, other arithmetic  4.24 us
    dot_general x1, matrix products, on_device(): jnp.einsum('kr,req->keq', k_sin, real, precision=high)  2.09 us
  transfers between devices with their start and end apart: 1, of which 1 were waited for; matrix products, arithmetic and copies ran while one was open for 5% of the time, Pallas kernels for 0%

profile of v1, /device:TPU:0, one launch (start us, length us, event | category | flops | bytes accessed | tf_op | source)
XLA Modules:
  0.0 101.4 jit_solution(10782819077773584544)
XLA Ops:
  6.6 1.5 %fusion.37 = (bf16[128,2,2,128]{3,2,1,0:T(2,128)(2,1)S(1)}, bf16[128,2,2,128]{3,2,1,0:T(2,128)(2,1)S(1)}, bf16[128,2,2,128]{3,2,1,0:T(2,128)(2,1)S(1)}, bf16[128,2,2,128]{3,2,1,0:T(2,128)(2,1)S(1)}) fusion(bf16[128,2,2,512]{3,2,1,0:T(2,128)(2,1)} %param.6), kind=kLoop, calls=%fused_computation.52 | loop fusion | bytes 1048576 | tf_op jit(solution)/shard_map/split | solution.py:37
  8.1 0.1 copy.47
  8.2 0.1 copy.48
  8.3 0.1 copy.49
  8.5 0.1 copy.50
  8.6 0.1 pad_maximum_fusion
  8.7 20.7 %all_to_all.5 = bf16[4,128,2,2,128]{1,4,3,2,0:T(8,128)(2,1)} all-to-all(bf16[4,128,2,2,128]{1,4,3,2,0:T(8,128)(2,1)S(1)} %pad_maximum_fusion), channel_id=1, replica_groups=mesh['blk'=8,'wide'=4] {'wide'}, dimensions={0} | all-to-all | bytes 1048576 | tf_op jit(solution)/shard_map/all_to_all | solution.py:37
  29.5 9.0 %all-gather = s32[4,2,3]{2,1,0:T(2,128)S(1)} all-gather(s32[1,2,3]{2,1,0:T(2,128)S(1)} %bitcast.46), channel_id=1, replica_groups=mesh['blk'=8,'wide'=4] {'wide'}, dimensions={0}, use_global_device_ids=true | all-gather | bytes 120 | tf_op jit(solution)/shard_map/all_gather | solution.py:40
  38.5 0.1 copy.37
  38.6 0.1 copy.36
  38.7 0.1 multiply_reduce_fusion.1
  38.9 0.3 multiply_reduce_fusion
  39.2 0.3 fusion.19
  39.5 4.2 %cosine_convert_fusion = (bf16[256,1024]{1,0:T(8,128)(2,1)S(1)}, bf16[256,1024]{1,0:T(8,128)(2,1)S(1)}) fusion(s32[256,1024]{1,0:T(8,128)S(1)} %multiply_reduce_fusion), kind=kLoop, calls=%fused_computation.22 | loop fusion | flops 3932160 | bytes 2097152 | tf_op jit(solution)/shard_map/convert
  43.7 22.4 %all-gather.3.cloned.1.call-done = bf16[1024,2048]{0,1:T(8,128)(2,1)} async-done(((bf16[128,2048]{0,1:T(8,128)(2,1)}), bf16[1024,2048]{0,1:T(8,128)(2,1)}) %all-gather.3.cloned.1.call-update) | async-done | bytes 4194320 | tf_op jit(solution)/shard_map/all_gather | solution.py:47
  66.1 6.6 %fusion.5 = f32[2048,512]{1,0:T(8,128)} fusion(bf16[1024,2048]{0,1:T(8,128)(2,1)} %all-gather.3.cloned.1.call-done, bf16[256,1024]{1,0:T(8,128)(2,1)S(1)} %get-tuple-element.12, bf16[256,1024]{1,0:T(8,128)(2,1)S(1)} %get-tuple-element.11), kind=kOutput, calls=%fused_computation.11 | convolution fusion | flops 2149580800 | bytes 9437184 | tf_op jit(solution)/shard_map/dot_general | solution.py:46
  72.7 5.9 %reshape.29 = f32[8,2,128,2,256]{4,3,2,1,0:T(2,128)} reshape(f32[2048,512]{1,0:T(8,128)} %fusion.5) | data formatting | bytes 8388608 | tf_op jit(solution)/shard_map/reshape | solution.py:52
  78.5 6.6 %fusion.36 = (f32[8,1,128,1,256]{4,3,2,1,0:T(1,128)S(1)}, f32[8,1,128,1,256]{4,3,2,1,0:T(1,128)S(1)}, f32[8,1,128,1,256]{4,3,2,1,0:T(1,128)S(1)}, f32[8,1,128,1,256]{4,3,2,1,0:T(1,128)S(1)}) fusion(f32[8,2,128,2,256]{4,3,2,1,0:T(2,128)} %reshape.29), kind=kLoop, calls=%fused_computation.51 | loop fusion | bytes 8388608 | tf_op jit(solution)/shard_map/slice | solution.py:53
  85.1 2.1 %fusion.14 = f32[2,128,256]{2,0,1:T(2,128)S(1)} fusion(f32[8,1,128,1,256]{4,3,2,1,0:T(1,128)S(1)} %get-tuple-element.9, f32[8,1,128,1,256]{4,3,2,1,0:T(1,128)S(1)} %get-tuple-element.7, f32[128,256]{1,0:T(8,128)S(1)} %fusion.19, f32[2,8]{1,0:T(2,128)S(1)} %cos.6), kind=kOutput, calls=%fused_computation.25 | convolution fusion | flops 6815744 | bytes 2490432 | tf_op jit(solution)/shard_map/kr,req->keq/dot_general | solution.py:59
  87.2 2.1 %fusion.16 = f32[2,128,256]{2,0,1:T(2,128)S(1)} fusion(f32[8,1,128,1,256]{4,3,2,1,0:T(1,128)S(1)} %get-tuple-element.10, f32[8,1,128,1,256]{4,3,2,1,0:T(1,128)S(1)} %get-tuple-element.8, f32[128,256]{1,0:T(8,128)S(1)} %fusion.19, f32[2,8]{1,0:T(2,128)S(1)} %cos.6), kind=kOutput, calls=%fused_computation.26 | convolution fusion | flops 6815744 | bytes 2490432 | tf_op jit(solution)/shard_map/kr,req->keq/dot_general | solution.py:62
  89.3 2.1 %fusion.1 = f32[2,1,128,256]{3,0,2,1:T(2,128)S(1)} fusion(f32[2,128,256]{2,0,1:T(2,128)S(1)} %fusion.14, f32[8,1,128,1,256]{4,3,2,1,0:T(1,128)S(1)} %get-tuple-element.10, f32[8,1,128,1,256]{4,3,2,1,0:T(1,128)S(1)} %get-tuple-element.8, f32[128,256]{1,0:T(8,128)S(1)} %fusion.19, f32[2,8]{1,0:T(2,128)S(1)} %get-tuple-element.5), kind=kOutput, calls=%fused_computation.7 | convolution fusion | flops 6881280 | bytes 2752576 | tf_op jit(solution)/shard_map/kr,req->keq/dot_general | solution.py:59
  91.4 2.1 %fusion = f32[2,1,128,256]{3,0,2,1:T(2,128)S(1)} fusion(f32[2,128,256]{2,0,1:T(2,128)S(1)} %fusion.16, f32[8,1,128,1,256]{4,3,2,1,0:T(1,128)S(1)} %get-tuple-element.9, f32[8,1,128,1,256]{4,3,2,1,0:T(1,128)S(1)} %get-tuple-element.7, f32[128,256]{1,0:T(8,128)S(1)} %fusion.19, f32[2,8]{1,0:T(2,128)S(1)} %get-tuple-element.5), kind=kOutput, calls=%fused_computation.5 | convolution fusion | flops 6881280 | bytes 2752576 | tf_op jit(solution)/shard_map/kr,req->keq/dot_general | solution.py:62
  93.5 0.2 pad_maximum_fusion.1
  93.7 0.8 copy.46
  (15 shorter events, 0.2 us)
Async XLA Ops:
  6.5 22.9 %copy-start.3 = (s32[3,2]{0,1:T(2,128)S(1)}, s32[3,2]{0,1:T(2,128)}, u32[]{:S(2)}) copy-start(s32[3,2]{0,1:T(2,128)} %param.8) | copy-start | bytes 76
  6.5 32.1 %copy-start.4 = (s32[3,2]{0,1:T(2,128)S(1)}, s32[3,2]{0,1:T(2,128)}, u32[]{:S(2)}) copy-start(s32[3,2]{0,1:T(2,128)} %param.10) | copy-start | bytes 76
  6.5 32.3 %copy-start = (s32[3,1024]{1,0:T(4,128)S(1)}, s32[3,1024]{1,0:T(4,128)}, u32[]{:S(2)}) copy-start(s32[3,1024]{1,0:T(4,128)} %param.7) | copy-start | bytes 36868
  6.5 32.4 %copy-start.2 = (s32[3,256]{1,0:T(4,128)S(1)}, s32[3,256]{1,0:T(4,128)}, u32[]{:S(2)}) copy-start(s32[3,256]{1,0:T(4,128)} %param.9) | copy-start | bytes 9220
  6.5 32.7 %copy-start.1 = (f32[16,256]{1,0:T(8,128)S(1)}, f32[16,256]{1,0:T(8,128)}, u32[]{:S(2)}) copy-start(f32[16,256]{1,0:T(8,128)} %param.11) | copy-start | bytes 49156
  6.5 59.5 %all-gather.3.cloned.1.call-start = ((), (), s32[]{:S(2)}) async-start(), calls=%async_computation.1 | async-start | bytes 4718592 | tf_op jit(solution)/shard_map/all_gather | solution.py:47
Sparse Core Ops, SparseCore 0:
  29.6 36.4 all-gather.2
